TPU v7x, 256 devices: a whole 4x4x8 slice. The times are simulated.
256 devices in a mesh: seq: 64 (over y, z, core), ch: 4 (over x).
Axes of the slice: x: 4, y: 4, z: 8, core: 2. Of those that a mesh axis runs over, the one named last changes fastest.
Arguments:
- features: bfloat16 [32768, 1024], P('seq', 'ch'), may hold values from -6 to 6
- w_in: bfloat16 [1024, 3, 1024], P(None, None, 'ch'), may hold values from -0.1875 to 0.1875
- bias_skip: float32 [1024], P('ch'), may hold values from -3 to 3
- filters: float32 [32768, 1024], P('seq', 'ch')
- w_out: bfloat16 [1024, 1024], P(None, 'ch'), may hold values from -0.1875 to 0.1875
- w_emb: bfloat16 [1024, 128], P('ch'), may hold values from -0.1875 to 0.1875
- page_lengths: int32 [512], replicated, may hold values from 1 to 256, 32768 in all
- page_owner: int32 [512], replicated, may hold values from 0 to 63
Outputs:
- index_rows: bfloat16 [32768, 128], P('seq')
Inputs may be any that keep to these rules, and one draw needn't show every extreme that they name: page_lengths sum to 32768, and the longest page has exactly 256 patches.
All inputs are finite; a program needn't handle non-finite values.
Results may differ from a plain program's by a relative error of at most 0.0057.
Values may be sent and summed in bfloat16 or wider, within the bound.
A program may use at most 64 MiB of HBM per device.

v0:
```python
import math
import jax
import jax.numpy as jnp
from jax import lax
from jax.sharding import PartitionSpec as P


def angle_table(first_index, second_index, period):
    product = first_index[:, None] * second_index[None, :] % period
    return product.astype(jnp.float32) * (2.0 * math.pi / period)


def apply_table(table, values):
    return jnp.einsum("ki,qic->qkc", table, values, precision=lax.Precision.HIGHEST)


def long_convolution(signal, filters, seq_count, seq_rank):
    rows_dev, chan_dev = signal.shape
    group_rows = rows_dev // seq_count
    block_count = 2 * seq_count
    fft_length = block_count * rows_dev
    block_index = jnp.arange(block_count, dtype=jnp.int32)
    source_index = jnp.arange(seq_count, dtype=jnp.int32)
    outer_angle = angle_table(block_index, source_index, block_count)
    outer_cos = jnp.cos(outer_angle)
    outer_sin = jnp.sin(outer_angle)
    local_rows = seq_rank * group_rows + jnp.arange(group_rows, dtype=jnp.int32)
    twist_angle = angle_table(block_index, local_rows, fft_length)
    twist_cos = jnp.cos(twist_angle)[:, :, None]
    twist_sin = jnp.sin(twist_angle)[:, :, None]
    inner_index = jnp.arange(rows_dev, dtype=jnp.int32)
    inner_angle = angle_table(inner_index, inner_index, rows_dev)
    inner_cos = jnp.cos(inner_angle)
    inner_sin = jnp.sin(inner_angle)
    signal_blocks, filter_blocks = (
        lax.all_to_all(
            signal.reshape(seq_count, group_rows, chan_dev),
            "seq",
            split_axis=0,
            concat_axis=0,
            tiled=True,
        ),
        lax.all_to_all(
            filters.reshape(seq_count, group_rows, chan_dev),
            "seq",
            split_axis=0,
            concat_axis=0,
            tiled=True,
        ),
    )

    def outer_forward(blocks):
        real_part = jnp.einsum("kj,jic->kic", outer_cos, blocks, precision=lax.Precision.HIGHEST)
        imag_part = -jnp.einsum("kj,jic->kic", outer_sin, blocks, precision=lax.Precision.HIGHEST)
        return jnp.stack(
            [
                real_part * twist_cos + imag_part * twist_sin,
                imag_part * twist_cos - real_part * twist_sin,
            ]
        )

    signal_spec, filter_spec = (
        lax.all_to_all(
            outer_forward(signal_blocks), "seq", split_axis=1, concat_axis=2, tiled=True
        ),
        lax.all_to_all(
            outer_forward(filter_blocks), "seq", split_axis=1, concat_axis=2, tiled=True
        ),
    )

    def inner_forward(spectrum):
        real_in = spectrum[0]
        imag_in = spectrum[1]
        return (
            apply_table(inner_cos, real_in) + apply_table(inner_sin, imag_in),
            apply_table(inner_cos, imag_in) - apply_table(inner_sin, real_in),
        )

    signal_real, signal_imag = inner_forward(signal_spec)
    filter_real, filter_imag = inner_forward(filter_spec)
    product_real = signal_real * filter_real - signal_imag * filter_imag
    product_imag = signal_real * filter_imag + signal_imag * filter_real
    back_real = apply_table(inner_cos, product_real) - apply_table(inner_sin, product_imag)
    back_imag = apply_table(inner_cos, product_imag) + apply_table(inner_sin, product_real)
    returned = lax.all_to_all(
        jnp.stack([back_real, back_imag]), "seq", split_axis=2, concat_axis=1, tiled=True
    )
    turned_real = returned[0] * twist_cos - returned[1] * twist_sin
    turned_imag = returned[0] * twist_sin + returned[1] * twist_cos
    result = (
        jnp.einsum("kj,kic->jic", outer_cos, turned_real, precision=lax.Precision.HIGHEST)
        - jnp.einsum("kj,kic->jic", outer_sin, turned_imag, precision=lax.Precision.HIGHEST)
    ) / fft_length
    back_tokens = lax.all_to_all(result, "seq", split_axis=0, concat_axis=1, tiled=True)
    return back_tokens.reshape(rows_dev, chan_dev)


def source_tokens(page_lengths, page_owner, output_rows):
    page_index = jnp.arange(page_lengths.shape[0], dtype=jnp.int32)
    before = (page_owner[None, :] < page_owner[:, None]) | (
        page_owner[None, :] == page_owner[:, None]
    ) & (page_index[None, :] < page_index[:, None])
    placed_start = jnp.sum(jnp.where(before, page_lengths[None, :], 0), axis=1)
    page_start = jnp.cumsum(page_lengths) - page_lengths
    inside = (output_rows[:, None] >= placed_start[None, :]) & (
        output_rows[:, None] < (placed_start + page_lengths)[None, :]
    )
    offsets = page_start[None, :] + output_rows[:, None] - placed_start[None, :]
    return jnp.sum(jnp.where(inside, offsets, 0), axis=1)


def body(features, w_in, bias_skip, filters, w_out, w_emb, page_lengths, page_owner):
    rows_dev, chan_dev = features.shape
    seq_count = lax.axis_size("seq")
    seq_rank = lax.axis_index("seq")
    flat_in = w_in.reshape(w_in.shape[0], -1)
    weight_rows = flat_in
    projected = jnp.dot(
        lax.all_gather(features, "ch", axis=1, tiled=True),
        weight_rows,
        preferred_element_type=jnp.float32,
    )
    projected = projected.reshape(rows_dev, 3, chan_dev)
    gate_branch = projected[:, 0]
    signal = projected[:, 1] * projected[:, 2]
    convolved = long_convolution(signal, filters, seq_count, seq_rank)
    mixed = ((convolved + bias_skip[None, :] * signal) * gate_branch).astype(jnp.bfloat16)
    weight_rows = w_out
    summed = jnp.dot(
        lax.all_gather(mixed, "ch", axis=1, tiled=True),
        weight_rows,
        preferred_element_type=jnp.float32,
    )
    layer_out = (summed + features.astype(jnp.float32)).astype(jnp.bfloat16)
    output_rows = seq_rank * rows_dev + jnp.arange(rows_dev, dtype=jnp.int32)
    source = source_tokens(page_lengths, page_owner, output_rows)
    embedded = lax.psum(jnp.dot(layer_out, w_emb, preferred_element_type=jnp.float32), "ch").astype(
        jnp.bfloat16
    )
    shard_part = lax.all_gather(embedded, "seq", axis=0, tiled=True)
    count_rows = shard_part.shape[0]
    inside = (source >= 0) & (source < count_rows)
    taken = jnp.take(shard_part, jnp.clip(source, 0, count_rows - 1), axis=0)
    return jnp.where(inside[:, None], taken, jnp.zeros_like(embedded))


def solution(mesh):
    return jax.shard_map(
        body,
        mesh=mesh,
        in_specs=(
            P("seq", "ch"),
            P(None, None, "ch"),
            P("ch"),
            P("seq", "ch"),
            P(None, "ch"),
            P("ch", None),
            P(),
            P(),
        ),
        out_specs=P("seq", None),
        check_vma=False,
    )
```

profile of v0, /device:TPU:1, one launch (start us, length us, event | category | flops | bytes accessed | tf_op | source)
XLA Modules:
  0.0 488.9 jit_solution(5704225290694879429)
XLA Ops:
  7.3 13.2 %all-to-all-start.2 = ((f32[64,8,256]{2,1,0:T(8,128)}), f32[64,8,256]{2,1,0:T(8,128)S(1)}, u32[]{:S(2)}, u32[]{:S(2)}) async-start(f32[64,8,256]{2,1,0:T(8,128)} %bitcast.145), calls=%async_computation.2 | async-start | bytes 1048576 | tf_op jit(solution)/shard_map/all_to_all | solution.py:43
  22.1 17.4 %all-gather.4.cloned.1.call-done = bf16[512,1024]{1,0:T(8,128)(2,1)} async-done(((bf16[512,256]{1,0:T(8,128)(2,1)}), bf16[512,1024]{1,0:T(8,128)(2,1)}) %all-gather.4.cloned.1.call-update) | async-done | bytes 1048592 | tf_op jit(solution)/shard_map/all_gather | solution.py:119
  39.6 2.2 fusion
  43.9 12.0 %all-to-all-start = ((f32[64,8,256]{2,1,0:T(8,128)}), f32[64,8,256]{2,1,0:T(8,128)S(1)}, u32[]{:S(2)}, u32[]{:S(2)}) async-start(f32[64,8,256]{2,1,0:T(8,128)} %fusion.89), calls=%async_computation | async-start | bytes 1048576 | tf_op jit(solution)/shard_map/all_to_all | solution.py:36
  59.4 13.8 %all-to-all-done = f32[64,8,256]{2,1,0:T(8,128)S(1)} async-done(((f32[64,8,256]{2,1,0:T(8,128)}), f32[64,8,256]{2,1,0:T(8,128)S(1)}, u32[]{:S(2)}, u32[]{:S(2)}) %all-to-all-start) | async-done | bytes 524320 | tf_op jit(solution)/shard_map/all_to_all | solution.py:36
  74.4 2.9 add_bitcast_fusion
  77.5 2.5 copy.64
  80.0 6.8 %all-to-all-start.3 = ((f32[2,128,8,256]{3,2,0,1:T(8,128)}), f32[2,128,8,256]{3,2,0,1:T(8,128)S(1)}, u32[]{:S(2)}, u32[]{:S(2)}) async-start(f32[2,128,8,256]{3,2,0,1:T(8,128)} %copy.64), calls=%async_computation.3 | async-start | bytes 4194304 | tf_op jit(solution)/shard_map/all_to_all | solution.py:66
  88.5 2.6 copy.56
  91.0 46.9 %all-to-all-done.3 = f32[2,128,8,256]{3,2,0,1:T(8,128)S(1)} async-done(((f32[2,128,8,256]{3,2,0,1:T(8,128)}), f32[2,128,8,256]{3,2,0,1:T(8,128)S(1)}, u32[]{:S(2)}, u32[]{:S(2)}) %all-to-all-start.3) | async-done | bytes 2097184 | tf_op jit(solution)/shard_map/all_to_all | solution.py:66
  139.3 5.8 %all-to-all-start.1 = ((f32[2,128,8,256]{3,2,0,1:T(8,128)}), f32[2,128,8,256]{3,2,0,1:T(8,128)S(1)}, u32[]{:S(2)}, u32[]{:S(2)}) async-start(f32[2,128,8,256]{3,2,0,1:T(8,128)} %copy.56), calls=%async_computation.1 | async-start | bytes 4194304 | tf_op jit(solution)/shard_map/all_to_all | solution.py:63
  147.0 7.2 %fusion.16 = f32[2,256,512]{2,1,0:T(8,128)S(1)} fusion(f32[1,2,64,8,256]{4,3,1,2,0:T(8,128)S(1)} %get-tuple-element.13), kind=kOutput, calls=%fused_computation.34 | convolution fusion | flops 1614282752 | bytes 2097152 | tf_op jit(solution)/shard_map/ki,qic->qkc/dot_general | solution.py:14
  154.2 7.4 %fusion.20 = f32[2,256,512]{2,1,0:T(8,128)S(1)} fusion(f32[1,2,64,8,256]{4,3,1,2,0:T(8,128)S(1)} %get-tuple-element.14), kind=kOutput, calls=%fused_computation.38 | convolution fusion | flops 1614282752 | bytes 2097152 | tf_op jit(solution)/shard_map/ki,qic->qkc/dot_general | solution.py:14
  161.6 8.1 %convolution_subtract_fusion.1 = f32[2,256,512]{2,1,0:T(8,128)} fusion(f32[2,256,512]{2,1,0:T(8,128)S(1)} %fusion.16, f32[1,2,64,8,256]{4,3,1,2,0:T(8,128)S(1)} %get-tuple-element.14), kind=kOutput, calls=%fused_computation.16 | convolution fusion | flops 1614544896 | bytes 3145728 | tf_op jit(solution)/shard_map/ki,qic->qkc/dot_general | solution.py:14
  169.7 8.3 %convolution_add_fusion.1 = f32[2,256,512]{2,1,0:T(8,128)} fusion(f32[2,256,512]{2,1,0:T(8,128)S(1)} %fusion.20, f32[1,2,64,8,256]{4,3,1,2,0:T(8,128)S(1)} %get-tuple-element.13), kind=kOutput, calls=%fused_computation.18 | convolution fusion | flops 1614544896 | bytes 3145728 | tf_op jit(solution)/shard_map/ki,qic->qkc/dot_general | solution.py:14
  178.0 18.3 %all-to-all-done.1 = f32[2,128,8,256]{3,2,0,1:T(8,128)S(1)} async-done(((f32[2,128,8,256]{3,2,0,1:T(8,128)}), f32[2,128,8,256]{3,2,0,1:T(8,128)S(1)}, u32[]{:S(2)}, u32[]{:S(2)}) %all-to-all-start.1) | async-done | bytes 2097184 | tf_op jit(solution)/shard_map/all_to_all | solution.py:63
  196.6 7.2 %fusion.36 = f32[2,256,512]{2,1,0:T(8,128)S(1)} fusion(f32[1,2,64,8,256]{4,3,1,2,0:T(8,128)S(1)} %get-tuple-element.15), kind=kOutput, calls=%fused_computation.54 | convolution fusion | flops 1614282752 | bytes 2097152 | tf_op jit(solution)/shard_map/ki,qic->qkc/dot_general | solution.py:14
  203.8 7.6 %fusion.28 = f32[2,256,512]{2,1,0:T(8,128)S(1)} fusion(f32[1,2,64,8,256]{4,3,1,2,0:T(8,128)S(1)} %get-tuple-element.16), kind=kOutput, calls=%fused_computation.46 | convolution fusion | flops 1614282752 | bytes 2097152 | tf_op jit(solution)/shard_map/ki,qic->qkc/dot_general | solution.py:14
  211.4 7.2 %convolution_add_fusion.2 = f32[2,256,512]{2,1,0:T(8,128)S(1)} fusion(f32[2,256,512]{2,1,0:T(8,128)S(1)} %fusion.36, f32[1,2,64,8,256]{4,3,1,2,0:T(8,128)S(1)} %get-tuple-element.16), kind=kOutput, calls=%fused_computation.19 | convolution fusion | flops 1614544896 | bytes 3145728 | tf_op jit(solution)/shard_map/ki,qic->qkc/dot_general | solution.py:14
  218.6 7.6 %multiply_subtract_fusion = (f32[2,256,512]{2,1,0:T(8,128)S(1)}, f32[2,256,512]{2,1,0:T(8,128)S(1)}) fusion(f32[2,256,512]{2,1,0:T(8,128)S(1)} %copy-done.5, f32[2,256,512]{2,1,0:T(8,128)S(1)} %convolution_add_fusion.2, f32[2,256,512]{2,1,0:T(8,128)S(1)} %copy-done.6, f32[2,256,512]{2,1,0:T(8,128)S(1)} %fusion.28, ...), kind=kOutput, calls=%fused_computation.67 | convolution fusion | flops 1616117760 | bytes 7340032 | tf_op jit(solution)/shard_map/ki,qic->qkc/dot_general | solution.py:14
  226.2 6.3 %fusion.14 = f32[2,256,512]{2,1,0:T(8,128)S(1)} fusion(f32[2,256,512]{2,1,0:T(8,128)S(1)} %get-tuple-element.5), kind=kOutput, calls=%fused_computation.32 | convolution fusion | flops 1614282752 | bytes 2097152 | tf_op jit(solution)/shard_map/ki,qic->qkc/dot_general | solution.py:14
  232.6 6.5 %fusion.10 = f32[2,256,512]{2,1,0:T(8,128)S(1)} fusion(f32[2,256,512]{2,1,0:T(8,128)S(1)} %get-tuple-element.6), kind=kOutput, calls=%fused_computation.28 | convolution fusion | flops 1614282752 | bytes 2097152 | tf_op jit(solution)/shard_map/ki,qic->qkc/dot_general | solution.py:14
  239.1 6.3 %fusion.3 = f32[1,2,512,256]{2,3,1,0:T(8,128)S(1)} fusion(f32[2,256,512]{2,1,0:T(8,128)S(1)} %fusion.14, f32[2,256,512]{2,1,0:T(8,128)S(1)} %get-tuple-element.6), kind=kOutput, calls=%fused_computation.15 | convolution fusion | flops 1614544896 | bytes 3145728 | tf_op jit(solution)/shard_map/ki,qic->qkc/dot_general | solution.py:14
  245.5 6.3 %fusion.2 = f32[1,2,512,256]{2,3,1,0:T(8,128)S(1)} fusion(f32[2,256,512]{2,1,0:T(8,128)S(1)} %fusion.10, f32[2,256,512]{2,1,0:T(8,128)S(1)} %get-tuple-element.5), kind=kOutput, calls=%fused_computation.13 | convolution fusion | flops 1614544896 | bytes 3145728 | tf_op jit(solution)/shard_map/ki,qic->qkc/dot_general | solution.py:14
  252.0 2.5 copy.74
  254.5 57.4 %all_to_all.64 = f32[2,2,512,256]{3,1,0,2:T(2,128)S(1)} all-to-all(f32[2,2,512,256]{3,1,0,2:T(2,128)} %copy.74), channel_id=1, replica_groups=mesh['seq'=64,'ch'=4] {'seq'}, dimensions={2} | all-to-all | bytes 4194304 | tf_op jit(solution)/shard_map/all_to_all | solution.py:85
  314.9 3.0 copy.77
  322.2 23.0 %all_to_all.65 = f32[64,8,256]{2,1,0:T(8,128)S(1)} all-to-all(f32[64,8,256]{2,1,0:T(8,128)S(1)} %copy.78), channel_id=1, replica_groups=mesh['seq'=64,'ch'=4] {'seq'}, dimensions={0} | all-to-all | bytes 1048576 | tf_op jit(solution)/shard_map/all_to_all | solution.py:94
  346.1 23.0 %all-gather.6.cloned.1.call-done = bf16[512,1024]{1,0:T(8,128)(2,1)} async-done(((bf16[512,256]{1,0:T(8,128)(2,1)}), bf16[512,1024]{1,0:T(8,128)(2,1)}) %all-gather.6.cloned.1.call-update) | async-done | bytes 1048592 | tf_op jit(solution)/shard_map/all_gather | solution.py:130
  371.0 15.8 %all-reduce.1 = bf16[512,128]{1,0:T(8,128)(2,1)} all-reduce(f32[512,128]{1,0:T(8,128)S(1)} %fusion.6), channel_id=1, replica_groups=mesh['seq'=64,'ch'=4] {'ch'}, use_global_device_ids=true, to_apply=%region_4.5 | all-reduce | flops 65536 | bytes 393216 | tf_op jit(solution)/shard_map/psum | solution.py:137
  388.2 87.3 %all-gather.8.cloned.1.call-done = bf16[32768,128]{1,0:T(8,128)(2,1)} async-done(((bf16[512,128]{1,0:T(8,128)(2,1)}), bf16[32768,128]{1,0:T(8,128)(2,1)}) %all-gather.8.cloned.1.call-update) | async-done | bytes 8388624 | tf_op jit(solution)/shard_map/all_gather | solution.py:140
  475.5 5.5 %gather_fusion = bf16[512,128]{1,0:T(8,128)(2,1)S(1)} fusion(bf16[32768,128]{1,0:T(8,128)(2,1)} %all-gather.8.cloned.1.call-done, s32[1024]{0:T(1024)S(1)} %pad_clamp_fusion), kind=kCustom, calls=%fused_computation | custom fusion | bytes 264192 | tf_op jit(solution)/shard_map/jit(_take)/gather | solution.py:143
  (67 shorter events, 27.1 us)
Async XLA Ops:
  6.5 362.6 %copy-start = (bf16[1024,256]{1,0:T(8,128)(2,1)S(1)}, bf16[1024,256]{1,0:T(8,128)(2,1)}, u32[]{:S(2)}) copy-start(bf16[1024,256]{1,0:T(8,128)(2,1)} %param.12) | copy-start | bytes 1572868
  6.5 33.0 %all-gather.4.cloned.1.call-start = ((), (), s32[]{:S(2)}) async-start(), calls=%async_computation.6 | async-start | bytes 1310720 | tf_op jit(solution)/shard_map/all_gather | solution.py:119
  7.3 36.6 %all-to-all-start.2 = ((f32[64,8,256]{2,1,0:T(8,128)}), f32[64,8,256]{2,1,0:T(8,128)S(1)}, u32[]{:S(2)}, u32[]{:S(2)}) async-start(f32[64,8,256]{2,1,0:T(8,128)} %bitcast.145), calls=%async_computation.2 | async-start | bytes 1048576 | tf_op jit(solution)/shard_map/all_to_all | solution.py:43
  41.8 1.2 copy-start.2
  43.9 29.3 %all-to-all-start = ((f32[64,8,256]{2,1,0:T(8,128)}), f32[64,8,256]{2,1,0:T(8,128)S(1)}, u32[]{:S(2)}, u32[]{:S(2)}) async-start(f32[64,8,256]{2,1,0:T(8,128)} %fusion.89), calls=%async_computation | async-start | bytes 1048576 | tf_op jit(solution)/shard_map/all_to_all | solution.py:36
  73.2 1.2 copy-start.4
  80.0 57.9 %all-to-all-start.3 = ((f32[2,128,8,256]{3,2,0,1:T(8,128)}), f32[2,128,8,256]{3,2,0,1:T(8,128)S(1)}, u32[]{:S(2)}, u32[]{:S(2)}) async-start(f32[2,128,8,256]{3,2,0,1:T(8,128)} %copy.64), calls=%async_computation.3 | async-start | bytes 4194304 | tf_op jit(solution)/shard_map/all_to_all | solution.py:66
  138.0 1.3 copy-start.1
  139.3 57.0 %all-to-all-start.1 = ((f32[2,128,8,256]{3,2,0,1:T(8,128)}), f32[2,128,8,256]{3,2,0,1:T(8,128)S(1)}, u32[]{:S(2)}, u32[]{:S(2)}) async-start(f32[2,128,8,256]{3,2,0,1:T(8,128)} %copy.56), calls=%async_computation.1 | async-start | bytes 4194304 | tf_op jit(solution)/shard_map/all_to_all | solution.py:63
  145.0 224.1 %all-gather.6.cloned.1.call-start = ((), (), s32[]{:S(2)}) async-start(), calls=%async_computation.7 | async-start | bytes 1310720 | tf_op jit(solution)/shard_map/all_gather | solution.py:130
  211.4 7.2 %copy-start.5 = (f32[2,256,512]{2,1,0:T(8,128)S(1)}, f32[2,256,512]{2,1,0:T(8,128)}, u32[]{:S(2)}) copy-start(f32[2,256,512]{2,1,0:T(8,128)} %convolution_subtract_fusion.1) | copy-start | bytes 3145732
  211.4 7.2 %copy-start.6 = (f32[2,256,512]{2,1,0:T(8,128)S(1)}, f32[2,256,512]{2,1,0:T(8,128)}, u32[]{:S(2)}) copy-start(f32[2,256,512]{2,1,0:T(8,128)} %convolution_add_fusion.1) | copy-start | bytes 3145732
  320.9 24.3 %copy-start.3 = (f32[512,3,256]{2,0,1:T(8,128)S(1)}, f32[512,3,256]{2,0,1:T(8,128)}, u32[]{:S(2)}) copy-start(f32[512,3,256]{2,0,1:T(8,128)} %copy-done.2) | copy-start | bytes 4718596
  320.9 24.3 %copy-start.10 = (f32[256]{0:T(256)S(1)}, f32[256]{0:T(256)}, u32[]{:S(2)}) copy-start(f32[256]{0:T(256)} %param.10) | copy-start | bytes 3076
  322.2 46.9 %copy-start.7 = (bf16[512,256]{1,0:T(8,128)(2,1)S(1)}, bf16[512,256]{1,0:T(8,128)(2,1)}, u32[]{:S(2)}) copy-start(bf16[512,256]{1,0:T(8,128)(2,1)} %param.8) | copy-start | bytes 786436
  322.2 46.9 %copy-start.11 = (bf16[256,128]{1,0:T(8,128)(2,1)S(1)}, bf16[256,128]{1,0:T(8,128)(2,1)}, u32[]{:S(2)}) copy-start(bf16[256,128]{1,0:T(8,128)(2,1)} %param.13) | copy-start | bytes 196612
  346.0 40.8 %copy-start.8 = (s32[512]{0:T(512)S(1)}, s32[512]{0:T(512)}, u32[]{:S(2)}) copy-start(s32[512]{0:T(512)} %param.14) | copy-start | bytes 6148
  346.0 41.3 %copy-start.9 = (s32[512]{0:T(512)S(1)}, s32[512]{0:T(512)}, u32[]{:S(2)}) copy-start(s32[512]{0:T(512)} %param.15) | copy-start | bytes 6148
  346.1 129.5 %all-gather.8.cloned.1.call-start = ((), (), s32[]{:S(2)}) async-start(), calls=%async_computation.8 | async-start | bytes 8519680 | tf_op jit(solution)/shard_map/all_gather | solution.py:140
Sparse Core Ops, SparseCore 0:
  9.1 30.3 all-gather.3
  346.2 22.8 all-gather.5
  386.9 88.5 all-gather.7
where the time goes:
time: 498 us; the launch traced here: 489 us
  waiting for transfers between devices  207 us (42%)
  matrix products  99.6 us (20%)
  blocking collectives  96.2 us (19%)
  starting transfers between devices  37.7 us (8%)
  local copies, waits for them, and re-layouts  28.1 us (6%)
  between operations  13.9 us (3%)
  other arithmetic  5.95 us (1%)
    all_gather x1, waiting for transfers between devices, body(): shard_part = lax.all_gather(embedded, 'seq', axis=0, tiled=True)  87.3 us
    dot_general x12, matrix products, apply_table(): jnp.einsum('ki,qic->qkc', table, values, precision=lax.Precision.HIGHEST)  86.1 us
    all_to_all x1, blocking collectives, long_convolution(): lax.all_to_all(jnp.stack([back_real, back_imag]), 'seq', split_axis=2, co...  57.4 us
    all_to_all x1, waiting for transfers between devices, long_convolution(): lax.all_to_all(outer_forward(filter_blocks), 'seq', split_axis=1, concat_...  46.9 us
    all_gather x1, waiting for transfers between devices, body(): lax.all_gather(mixed, 'ch', axis=1, tiled=True)  23 us
    all_to_all x1, blocking collectives, long_convolution(): lax.all_to_all(result, 'seq', split_axis=0, concat_axis=1, tiled=True)  23 us
    all_to_all x1, waiting for transfers between devices, long_convolution(): lax.all_to_all(outer_forward(signal_blocks), 'seq', split_axis=1, concat_...  18.3 us
    all_gather x1, waiting for transfers between devices, body(): lax.all_gather(features, 'ch', axis=1, tiled=True)  17.4 us
  transfers between devices with their start and end apart: 7, of which 6 were waited for; matrix products, arithmetic and copies ran while one was open for 10% of the time, Pallas kernels for 0%

commit v1 on v0

--- a/solution.py
+++ b/solution.py
@@ -3,6 +3,13 @@
 import jax.numpy as jnp
 from jax import lax
 from jax.sharding import PartitionSpec as P
+
+
+def all_by_exchange(x, mesh_axis, dim):
+    count = lax.axis_size(mesh_axis)
+    blocks = jnp.stack([x for _ in range(count)])
+    blocks = lax.all_to_all(blocks, mesh_axis, split_axis=0, concat_axis=0)
+    return jnp.concatenate(blocks, axis=dim)
 
 
 def angle_table(first_index, second_index, period):
@@ -137,7 +144,7 @@
     embedded = lax.psum(jnp.dot(layer_out, w_emb, preferred_element_type=jnp.float32), "ch").astype(
         jnp.bfloat16
     )
-    shard_part = lax.all_gather(embedded, "seq", axis=0, tiled=True)
+    shard_part = all_by_exchange(embedded, "seq", 0)
     count_rows = shard_part.shape[0]
     inside = (source >= 0) & (source < count_rows)
     taken = jnp.take(shard_part, jnp.clip(source, 0, count_rows - 1), axis=0)

time: 498 us -> 623 us (1.25)
  waiting for transfers between devices: 207 us -> 311 us
  starting transfers between devices: 37.7 us -> 53.9 us
    all_to_all x0 -> x1, waiting for transfers between devices: none -> 184 us  [all_by_exchange(): blocks = lax.all_to_all(blocks, mesh_axis, split_axis=0, concat_axis=0)]
    all_gather x1 -> x0, waiting for transfers between devices: 87.3 us -> none  [body(): shard_part = lax.all_gather(embedded, 'seq', axis=0, tiled=True)]
    all_to_all x0 -> x1, starting transfers between devices: none -> 16.4 us  [all_by_exchange(): blocks = lax.all_to_all(blocks, mesh_axis, split_axis=0, concat_axis=0)]
    all_to_all x1, waiting for transfers between devices: 18.3 us -> 25.3 us  [long_convolution(): lax.all_to_all(outer_forward(signal_blocks), 'seq', split_axis=1, concat_...]
  transfers between devices with their start and end apart: 7 -> 7, of which waited for: 6 -> 6; matrix products, arithmetic and copies ran while one was open for 10% -> 6% of each run, Pallas kernels for 0% -> 0%
where the time goes in v1:
time: 623 us; the launch traced here: 615 us
  waiting for transfers between devices  311 us (50%)
  matrix products  100 us (16%)
  blocking collectives  95.9 us (15%)
  starting transfers between devices  53.9 us (9%)
  local copies, waits for them, and re-layouts  33.4 us (5%)
  between operations  14.3 us (2%)
    all_to_all x1, waiting for transfers between devices, all_by_exchange(): blocks = lax.all_to_all(blocks, mesh_axis, split_axis=0, concat_axis=0)  184 us
    dot_general x12, matrix products, apply_table(): jnp.einsum('ki,qic->qkc', table, values, precision=lax.Precision.HIGHEST)  86.6 us
    all_to_all x1, blocking collectives, long_convolution(): lax.all_to_all(jnp.stack([back_real, back_imag]), 'seq', split_axis=2, co...  57 us
    all_to_all x1, waiting for transfers between devices, long_convolution(): lax.all_to_all(outer_forward(filter_blocks), 'seq', split_axis=1, concat_...  46.9 us
    all_to_all x1, waiting for transfers between devices, long_convolution(): lax.all_to_all(outer_forward(signal_blocks), 'seq', split_axis=1, concat_...  25.3 us
    all_to_all x1, blocking collectives, long_convolution(): lax.all_to_all(result, 'seq', split_axis=0, concat_axis=1, tiled=True)  23.5 us
    all_gather x1, waiting for transfers between devices, body(): lax.all_gather(mixed, 'ch', axis=1, tiled=True)  22.9 us
    all_gather x1, waiting for transfers between devices, body(): lax.all_gather(features, 'ch', axis=1, tiled=True)  17.4 us
  transfers between devices with their start and end apart: 7, of which 6 were waited for; matrix products, arithmetic and copies ran while one was open for 6% of the time, Pallas kernels for 0%

profile of v1, /device:TPU:1, one launch (start us, length us, event | category | flops | bytes accessed | tf_op | source)
XLA Modules:
  0.0 614.7 jit_solution(1548636594959899292)
XLA Ops:
  7.3 13.2 %all-to-all-start.2 = ((f32[64,8,256]{2,1,0:T(8,128)}), f32[64,8,256]{2,1,0:T(8,128)S(1)}, u32[]{:S(2)}, u32[]{:S(2)}) async-start(f32[64,8,256]{2,1,0:T(8,128)} %bitcast.146), calls=%async_computation.2 | async-start | bytes 1048576 | tf_op jit(solution)/shard_map/all_to_all | solution.py:50
  22.1 17.4 %all-gather.3.cloned.1.call-done = bf16[512,1024]{1,0:T(8,128)(2,1)} async-done(((bf16[512,256]{1,0:T(8,128)(2,1)}), bf16[512,1024]{1,0:T(8,128)(2,1)}) %all-gather.3.cloned.1.call-update) | async-done | bytes 1048592 | tf_op jit(solution)/shard_map/all_gather | solution.py:126
  43.9 12.0 %all-to-all-start = ((f32[64,8,256]{2,1,0:T(8,128)}), f32[64,8,256]{2,1,0:T(8,128)S(1)}, u32[]{:S(2)}, u32[]{:S(2)}) async-start(f32[64,8,256]{2,1,0:T(8,128)} %fusion.89), calls=%async_computation | async-start | bytes 1048576 | tf_op jit(solution)/shard_map/all_to_all | solution.py:43
  59.4 13.8 %all-to-all-done = f32[64,8,256]{2,1,0:T(8,128)S(1)} async-done(((f32[64,8,256]{2,1,0:T(8,128)}), f32[64,8,256]{2,1,0:T(8,128)S(1)}, u32[]{:S(2)}, u32[]{:S(2)}) %all-to-all-start) | async-done | bytes 524320 | tf_op jit(solution)/shard_map/all_to_all | solution.py:43
  74.4 2.9 add_bitcast_fusion
  77.5 2.5 copy.64
  80.0 6.6 %all-to-all-start.3 = ((f32[2,128,8,256]{3,2,0,1:T(8,128)}), f32[2,128,8,256]{3,2,0,1:T(8,128)S(1)}, u32[]{:S(2)}, u32[]{:S(2)}) async-start(f32[2,128,8,256]{3,2,0,1:T(8,128)} %copy.64), calls=%async_computation.3 | async-start | bytes 4194304 | tf_op jit(solution)/shard_map/all_to_all | solution.py:73
  88.3 2.6 copy.56
  90.9 46.9 %all-to-all-done.3 = f32[2,128,8,256]{3,2,0,1:T(8,128)S(1)} async-done(((f32[2,128,8,256]{3,2,0,1:T(8,128)}), f32[2,128,8,256]{3,2,0,1:T(8,128)S(1)}, u32[]{:S(2)}, u32[]{:S(2)}) %all-to-all-start.3) | async-done | bytes 2097184 | tf_op jit(solution)/shard_map/all_to_all | solution.py:73
  139.1 5.8 all-to-all-start.1
  146.9 7.2 %fusion.20 = f32[2,256,512]{2,1,0:T(8,128)S(1)} fusion(f32[1,2,64,8,256]{4,3,1,2,0:T(8,128)S(1)} %get-tuple-element.14), kind=kOutput, calls=%fused_computation.38 | convolution fusion | flops 1614282752 | bytes 2097152 | tf_op jit(solution)/shard_map/ki,qic->qkc/dot_general | solution.py:21
  154.1 8.5 %fusion.16 = f32[2,256,512]{2,1,0:T(8,128)} fusion(f32[1,2,64,8,256]{4,3,1,2,0:T(8,128)S(1)} %get-tuple-element.13), kind=kOutput, calls=%fused_computation.34 | convolution fusion | flops 1614282752 | bytes 2097152 | tf_op jit(solution)/shard_map/ki,qic->qkc/dot_general | solution.py:21
  162.6 8.2 %convolution_add_fusion.1 = f32[2,256,512]{2,1,0:T(8,128)} fusion(f32[2,256,512]{2,1,0:T(8,128)S(1)} %fusion.20, f32[1,2,64,8,256]{4,3,1,2,0:T(8,128)S(1)} %get-tuple-element.13), kind=kOutput, calls=%fused_computation.18 | convolution fusion | flops 1614544896 | bytes 3145728 | tf_op jit(solution)/shard_map/ki,qic->qkc/dot_general | solution.py:21
  170.8 25.3 %all-to-all-done.1 = f32[2,128,8,256]{3,2,0,1:T(8,128)S(1)} async-done(((f32[2,128,8,256]{3,2,0,1:T(8,128)}), f32[2,128,8,256]{3,2,0,1:T(8,128)S(1)}, u32[]{:S(2)}, u32[]{:S(2)}) %all-to-all-start.1) | async-done | bytes 2097184 | tf_op jit(solution)/shard_map/all_to_all | solution.py:70
  196.4 7.2 %fusion.36 = f32[2,256,512]{2,1,0:T(8,128)S(1)} fusion(f32[1,2,64,8,256]{4,3,1,2,0:T(8,128)S(1)} %get-tuple-element.15), kind=kOutput, calls=%fused_computation.54 | convolution fusion | flops 1614282752 | bytes 2097152 | tf_op jit(solution)/shard_map/ki,qic->qkc/dot_general | solution.py:21
  203.6 7.4 %fusion.28 = f32[2,256,512]{2,1,0:T(8,128)S(1)} fusion(f32[1,2,64,8,256]{4,3,1,2,0:T(8,128)S(1)} %get-tuple-element.16), kind=kOutput, calls=%fused_computation.46 | convolution fusion | flops 1614282752 | bytes 2097152 | tf_op jit(solution)/shard_map/ki,qic->qkc/dot_general | solution.py:21
  211.0 7.2 %convolution_add_fusion.2 = f32[2,256,512]{2,1,0:T(8,128)S(1)} fusion(f32[2,256,512]{2,1,0:T(8,128)S(1)} %fusion.36, f32[1,2,64,8,256]{4,3,1,2,0:T(8,128)S(1)} %get-tuple-element.16), kind=kOutput, calls=%fused_computation.19 | convolution fusion | flops 1614544896 | bytes 3145728 | tf_op jit(solution)/shard_map/ki,qic->qkc/dot_general | solution.py:21
  218.3 7.6 %convolution_subtract_fusion.1 = f32[2,256,512]{2,1,0:T(8,128)S(1)} fusion(f32[2,256,512]{2,1,0:T(8,128)S(1)} %copy-done.13, f32[1,2,64,8,256]{4,3,1,2,0:T(8,128)S(1)} %copy-done.7), kind=kOutput, calls=%fused_computation.16 | convolution fusion | flops 1614544896 | bytes 3145728 | tf_op jit(solution)/shard_map/ki,qic->qkc/dot_general | solution.py:21
  226.0 7.6 %multiply_subtract_fusion = (f32[2,256,512]{2,1,0:T(8,128)S(1)}, f32[2,256,512]{2,1,0:T(8,128)S(1)}) fusion(f32[2,256,512]{2,1,0:T(8,128)S(1)} %convolution_subtract_fusion.1, f32[2,256,512]{2,1,0:T(8,128)S(1)} %convolution_add_fusion.2, f32[2,256,512]{2,1,0:T(8,128)S(1)} %copy-done.5, f32[2,256,512]{2,1,0:T(8,128)S(1)} %fusion.28, ...), kind=kOutput, calls=%fused_computation.67 | convolution fusion | flops 1616117760 | bytes 7340032 | tf_op jit(solution)/shard_map/ki,qic->qkc/dot_general | solution.py:21
  233.6 6.3 %fusion.14 = f32[2,256,512]{2,1,0:T(8,128)S(1)} fusion(f32[2,256,512]{2,1,0:T(8,128)S(1)} %get-tuple-element.5), kind=kOutput, calls=%fused_computation.32 | convolution fusion | flops 1614282752 | bytes 2097152 | tf_op jit(solution)/shard_map/ki,qic->qkc/dot_general | solution.py:21
  239.9 6.3 %fusion.10 = f32[2,256,512]{2,1,0:T(8,128)S(1)} fusion(f32[2,256,512]{2,1,0:T(8,128)S(1)} %get-tuple-element.6), kind=kOutput, calls=%fused_computation.28 | convolution fusion | flops 1614282752 | bytes 2097152 | tf_op jit(solution)/shard_map/ki,qic->qkc/dot_general | solution.py:21
  246.2 6.3 %fusion.3 = f32[1,2,512,256]{2,3,1,0:T(8,128)S(1)} fusion(f32[2,256,512]{2,1,0:T(8,128)S(1)} %fusion.14, f32[2,256,512]{2,1,0:T(8,128)S(1)} %get-tuple-element.6), kind=kOutput, calls=%fused_computation.15 | convolution fusion | flops 1614544896 | bytes 3145728 | tf_op jit(solution)/shard_map/ki,qic->qkc/dot_general | solution.py:21
  252.6 6.6 %fusion.2 = f32[1,2,512,256]{2,3,1,0:T(8,128)S(1)} fusion(f32[2,256,512]{2,1,0:T(8,128)S(1)} %fusion.10, f32[2,256,512]{2,1,0:T(8,128)S(1)} %get-tuple-element.5), kind=kOutput, calls=%fused_computation.13 | convolution fusion | flops 1614544896 | bytes 3145728 | tf_op jit(solution)/shard_map/ki,qic->qkc/dot_general | solution.py:21
  261.8 57.0 %all_to_all.69 = f32[2,2,512,256]{3,1,0,2:T(2,128)S(1)} all-to-all(f32[2,2,512,256]{3,1,0,2:T(2,128)} %copy.74), channel_id=1, replica_groups=mesh['seq'=64,'ch'=4] {'seq'}, dimensions={2} | all-to-all | bytes 4194304 | tf_op jit(solution)/shard_map/all_to_all | solution.py:92
  321.9 3.0 copy.77
  329.2 23.5 %all_to_all.70 = f32[64,8,256]{2,1,0:T(8,128)S(1)} all-to-all(f32[64,8,256]{2,1,0:T(8,128)S(1)} %copy.78), channel_id=1, replica_groups=mesh['seq'=64,'ch'=4] {'seq'}, dimensions={0} | all-to-all | bytes 1048576 | tf_op jit(solution)/shard_map/all_to_all | solution.py:101
  353.5 22.9 %all-gather.5.cloned.1.call-done = bf16[512,1024]{1,0:T(8,128)(2,1)} async-done(((bf16[512,256]{1,0:T(8,128)(2,1)}), bf16[512,1024]{1,0:T(8,128)(2,1)}) %all-gather.5.cloned.1.call-update) | async-done | bytes 1048592 | tf_op jit(solution)/shard_map/all_gather | solution.py:137
  378.3 15.4 %all-reduce.1 = bf16[512,128]{1,0:T(8,128)(2,1)S(1)} all-reduce(f32[512,128]{1,0:T(8,128)S(1)} %fusion.6), channel_id=1, replica_groups=mesh['seq'=64,'ch'=4] {'ch'}, use_global_device_ids=true, to_apply=%region_4.5 | all-reduce | flops 65536 | bytes 393216 | tf_op jit(solution)/shard_map/psum | solution.py:144
  393.6 5.3 stack.29
  398.9 16.4 %all-to-all-start.6 = ((bf16[64,512,128]{2,1,0:T(8,128)(2,1)}), bf16[64,512,128]{2,1,0:T(8,128)(2,1)}, u32[]{:S(2)}, u32[]{:S(2)}) async-start(bf16[64,512,128]{2,1,0:T(8,128)(2,1)} %stack.29), calls=%async_computation.6 | async-start | bytes 16777216 | tf_op jit(solution)/shard_map/all_to_all | solution.py:11
  416.7 184.3 %all-to-all-done.6 = bf16[64,512,128]{2,1,0:T(8,128)(2,1)} async-done(((bf16[64,512,128]{2,1,0:T(8,128)(2,1)}), bf16[64,512,128]{2,1,0:T(8,128)(2,1)}, u32[]{:S(2)}, u32[]{:S(2)}) %all-to-all-start.6) | async-done | bytes 8388640 | tf_op jit(solution)/shard_map/all_to_all | solution.py:11
  601.0 5.5 gather_fusion
  (71 shorter events, 31.7 us)
Async XLA Ops:
  6.5 369.9 %copy-start = (bf16[1024,256]{1,0:T(8,128)(2,1)S(1)}, bf16[1024,256]{1,0:T(8,128)(2,1)}, u32[]{:S(2)}) copy-start(bf16[1024,256]{1,0:T(8,128)(2,1)} %param.12) | copy-start | bytes 1572868
  6.5 33.0 %all-gather.3.cloned.1.call-start = ((), (), s32[]{:S(2)}) async-start(), calls=%async_computation.7 | async-start | bytes 1310720 | tf_op jit(solution)/shard_map/all_gather | solution.py:126
  7.3 36.6 %all-to-all-start.2 = ((f32[64,8,256]{2,1,0:T(8,128)}), f32[64,8,256]{2,1,0:T(8,128)S(1)}, u32[]{:S(2)}, u32[]{:S(2)}) async-start(f32[64,8,256]{2,1,0:T(8,128)} %bitcast.146), calls=%async_computation.2 | async-start | bytes 1048576 | tf_op jit(solution)/shard_map/all_to_all | solution.py:50
  41.8 1.2 copy-start.2
  43.9 29.3 %all-to-all-start = ((f32[64,8,256]{2,1,0:T(8,128)}), f32[64,8,256]{2,1,0:T(8,128)S(1)}, u32[]{:S(2)}, u32[]{:S(2)}) async-start(f32[64,8,256]{2,1,0:T(8,128)} %fusion.89), calls=%async_computation | async-start | bytes 1048576 | tf_op jit(solution)/shard_map/all_to_all | solution.py:43
  73.2 1.2 copy-start.4
  80.0 57.8 %all-to-all-start.3 = ((f32[2,128,8,256]{3,2,0,1:T(8,128)}), f32[2,128,8,256]{3,2,0,1:T(8,128)S(1)}, u32[]{:S(2)}, u32[]{:S(2)}) async-start(f32[2,128,8,256]{3,2,0,1:T(8,128)} %copy.64), calls=%async_computation.3 | async-start | bytes 4194304 | tf_op jit(solution)/shard_map/all_to_all | solution.py:73
  137.8 1.3 copy-start.1
  139.1 57.0 %all-to-all-start.1 = ((f32[2,128,8,256]{3,2,0,1:T(8,128)}), f32[2,128,8,256]{3,2,0,1:T(8,128)S(1)}, u32[]{:S(2)}, u32[]{:S(2)}) async-start(f32[2,128,8,256]{3,2,0,1:T(8,128)} %copy.56), calls=%async_computation.1 | async-start | bytes 4194304 | tf_op jit(solution)/shard_map/all_to_all | solution.py:70
  144.9 231.5 %all-gather.5.cloned.1.call-start = ((), (), s32[]{:S(2)}) async-start(), calls=%async_computation.8 | async-start | bytes 1310720 | tf_op jit(solution)/shard_map/all_gather | solution.py:137
  146.8 7.2 %copy-start.6 = (f32[1,2,64,8,256]{4,3,1,2,0:T(8,128)}, f32[1,2,64,8,256]{4,3,1,2,0:T(8,128)S(1)}, u32[]{:S(2)}) copy-start(f32[1,2,64,8,256]{4,3,1,2,0:T(8,128)S(1)} %get-tuple-element.14) | copy-start | bytes 3145732
  211.0 7.3 %copy-start.7 = (f32[1,2,64,8,256]{4,3,1,2,0:T(8,128)S(1)}, f32[1,2,64,8,256]{4,3,1,2,0:T(8,128)}, u32[]{:S(2)}) copy-start(f32[1,2,64,8,256]{4,3,1,2,0:T(8,128)} %copy-done.6) | copy-start | bytes 3145732
  211.0 7.3 %copy-start.13 = (f32[2,256,512]{2,1,0:T(8,128)S(1)}, f32[2,256,512]{2,1,0:T(8,128)}, u32[]{:S(2)}) copy-start(f32[2,256,512]{2,1,0:T(8,128)} %fusion.16) | copy-start | bytes 3145732
  218.3 7.6 %copy-start.5 = (f32[2,256,512]{2,1,0:T(8,128)S(1)}, f32[2,256,512]{2,1,0:T(8,128)}, u32[]{:S(2)}) copy-start(f32[2,256,512]{2,1,0:T(8,128)} %convolution_add_fusion.1) | copy-start | bytes 3145732
  327.9 24.8 %copy-start.3 = (f32[512,3,256]{2,0,1:T(8,128)S(1)}, f32[512,3,256]{2,0,1:T(8,128)}, u32[]{:S(2)}) copy-start(f32[512,3,256]{2,0,1:T(8,128)} %copy-done.2) | copy-start | bytes 4718596
  327.9 24.8 %copy-start.11 = (f32[256]{0:T(256)S(1)}, f32[256]{0:T(256)}, u32[]{:S(2)}) copy-start(f32[256]{0:T(256)} %param.10) | copy-start | bytes 3076
  329.2 47.2 %copy-start.8 = (bf16[512,256]{1,0:T(8,128)(2,1)S(1)}, bf16[512,256]{1,0:T(8,128)(2,1)}, u32[]{:S(2)}) copy-start(bf16[512,256]{1,0:T(8,128)(2,1)} %param.8) | copy-start | bytes 786436
  329.2 47.2 %copy-start.12 = (bf16[256,128]{1,0:T(8,128)(2,1)S(1)}, bf16[256,128]{1,0:T(8,128)(2,1)}, u32[]{:S(2)}) copy-start(bf16[256,128]{1,0:T(8,128)(2,1)} %param.13) | copy-start | bytes 196612
  398.9 16.4 %copy-start.9 = (s32[512]{0:T(512)S(1)}, s32[512]{0:T(512)}, u32[]{:S(2)}) copy-start(s32[512]{0:T(512)} %param.14) | copy-start | bytes 6148
  398.9 16.9 %copy-start.10 = (s32[512]{0:T(512)S(1)}, s32[512]{0:T(512)}, u32[]{:S(2)}) copy-start(s32[512]{0:T(512)} %param.15) | copy-start | bytes 6148
  398.9 202.1 %all-to-all-start.6 = ((bf16[64,512,128]{2,1,0:T(8,128)(2,1)}), bf16[64,512,128]{2,1,0:T(8,128)(2,1)}, u32[]{:S(2)}, u32[]{:S(2)}) async-start(bf16[64,512,128]{2,1,0:T(8,128)(2,1)} %stack.29), calls=%async_computation.6 | async-start | bytes 16777216 | tf_op jit(solution)/shard_map/all_to_all | solution.py:11
Sparse Core Ops, SparseCore 0:
  9.1 30.3 all-gather.2
  353.7 22.7 all-gather.4
